TPU v7x, 512 devices: a whole 4x8x8 slice. The times are simulated.
512 devices in a mesh: ctx: 64 (over y, z), tp: 8 (over x, core).
Axes of the slice: x: 4, y: 8, z: 8, core: 2. Of those that a mesh axis runs over, the one named last changes fastest.
Arguments:
- inputs: bfloat16 [8192, 4096], P('ctx', 'tp'), may hold values from -6 to 6
- gate_in: bfloat16 [8192, 4096], P('ctx', 'tp'), may hold values from -6 to 6
- b_proj: bfloat16 [8192, 128], P('ctx'), may hold values from -0.5 to 0.5
- c_proj: bfloat16 [8192, 128], P('ctx'), may hold values from -0.5 to 0.5
- log_decay: float32 [32, 8192], P('tp', 'ctx'), may hold values from -0.75 to 0
- w_out: bfloat16 [4096, 4096], P('tp'), may hold values from -0.09375 to 0.09375
- cotangent: bfloat16 [8192, 4096], P(('ctx', 'tp')), may hold values from -6 to 6
Outputs:
- layer_out: bfloat16 [8192, 4096], P(('ctx', 'tp'))
- grad_inputs: bfloat16 [8192, 4096], P('ctx', 'tp')
- grad_gate: bfloat16 [8192, 4096], P('ctx', 'tp')
- grad_b: float32 [8192, 128], P(('ctx', 'tp'))
- grad_c: float32 [8192, 128], P(('ctx', 'tp'))
- grad_decay: float32 [32, 8192], P('tp', 'ctx')
All inputs are finite; a program needn't handle non-finite values.
Results may differ from a plain program's by a relative error of at most 0.017.
Values may be sent and summed in bfloat16 or wider, within the bound.
No kernel may reach another device: no remote copies, remote signals or barrier semaphores. Data moves between devices by JAX's collectives and lax.ppermute only.
A program may use at most 128 MiB of HBM per device.

v0:
```python
import jax
import jax.numpy as jnp
from jax import lax
from jax.sharding import PartitionSpec as P

BLOCK = 128


def entering(shard, axis, combine, identity, reverse):
    count, place = (lax.axis_size(axis), lax.axis_index(axis))
    everything = jax.tree.map(lambda part: lax.all_gather(part, axis), shard)
    start = jax.tree.map(
        lambda part, zero: jnp.broadcast_to(jnp.asarray(zero, part.dtype), part.shape),
        shard,
        identity,
    )

    def lap(k, before):
        at = count - 1 - k if reverse else k
        reached = at > place if reverse else at < place
        new = combine(before, jax.tree.map(lambda part: part[at], everything))
        return jax.tree.map(lambda a, b: jnp.where(reached, a, b), new, before)

    return lax.fori_loop(0, count, lap, start)


def compose(earlier, later_part):
    return (earlier[0] * later_part[0], later_part[0][:, None, None] * earlier[1] + later_part[1])


def carried(block_decay, block_terms, backward):
    if backward:
        block_decay = jnp.flip(block_decay, 0)
        block_terms = jnp.flip(block_terms, 0)
    head_count = block_decay.shape[1]

    def local_step(running, packed):
        state_level, product = running
        decay_step, term_block = packed
        return (
            (decay_step[:, None, None] * state_level + term_block, decay_step * product),
            (state_level, product),
        )

    initial = (jnp.zeros(block_terms.shape[1:], jnp.float32), jnp.ones((head_count,), jnp.float32))
    (dev_state, dev_decay), (local_in, decay_before) = lax.scan(
        local_step, initial, (block_decay, block_terms)
    )
    identity = (jnp.ones((head_count,), jnp.float32), jnp.zeros(block_terms.shape[1:], jnp.float32))
    if backward:
        incoming = entering((dev_decay, dev_state), "ctx", compose, identity, True)[1]
    else:
        incoming = entering((dev_decay, dev_state), "ctx", compose, identity, False)[1]

    def resume(state_level, packed):
        decay_step, term_block = packed
        return (decay_step[:, None, None] * state_level + term_block, state_level)

    unused, states = lax.scan(resume, incoming, (block_decay, block_terms))
    if backward:
        states = jnp.flip(states, 0)
    return states


def local(inputs, gate_in, b_proj, c_proj, log_decay, w_out, cotangent):
    tok_rows, feature_width = inputs.shape
    head_count = log_decay.shape[0]
    head_dim = feature_width // head_count
    nblocks = tok_rows // BLOCK
    nstate = b_proj.shape[1]
    x_blocks = inputs.reshape(nblocks, BLOCK, head_count, head_dim)
    b_blocks = b_proj.reshape(nblocks, BLOCK, nstate)
    c_blocks = c_proj.reshape(nblocks, BLOCK, nstate)
    d_blocks = jnp.transpose(log_decay.reshape(head_count, nblocks, BLOCK), (1, 2, 0))
    gate_float = gate_in.astype(jnp.float32).reshape(nblocks, BLOCK, head_count, head_dim)
    sigmoid_z = jax.nn.sigmoid(gate_float)
    silu_z = gate_float * sigmoid_z
    position = jnp.arange(BLOCK)
    causal = position[:, None] >= position[None, :]
    lower_ones = causal.astype(jnp.float32)
    cumulative = jnp.einsum("qs,csh->cqh", lower_ones, d_blocks, precision=lax.Precision.HIGHEST)
    final_sum = cumulative[:, -1, :]
    block_decay = jnp.exp(final_sum)
    tail_weight = jnp.exp(final_sum[:, None, :] - cumulative)
    exp_cum = jnp.exp(cumulative)
    column_cum = jnp.transpose(cumulative, (0, 2, 1))
    differ = column_cum[:, :, :, None] - column_cum[:, :, None, :]
    decay_mat = jnp.where(causal, jnp.exp(jnp.minimum(differ, 0.0)), 0.0)
    scores = jnp.einsum("cqn,ckn->cqk", c_blocks, b_blocks, preferred_element_type=jnp.float32)
    mixing_b = (scores[:, None] * decay_mat).astype(jnp.bfloat16)
    y_intra = jnp.einsum("chqk,ckhp->cqhp", mixing_b, x_blocks, preferred_element_type=jnp.float32)
    weighted = (x_blocks.astype(jnp.float32) * tail_weight[..., None]).astype(jnp.bfloat16)
    block_state = jnp.einsum(
        "cqhp,cqn->chpn", weighted, b_blocks, preferred_element_type=jnp.float32
    )
    state_in = carried(block_decay, block_state, False)
    state_b = state_in.astype(jnp.bfloat16)
    y_inter = (
        jnp.einsum("cqn,chpn->cqhp", c_blocks, state_b, preferred_element_type=jnp.float32)
        * exp_cum[..., None]
    )
    y_full = y_intra + y_inter
    gated_out = (y_full * silu_z).astype(jnp.bfloat16).reshape(tok_rows, feature_width)
    layer_out = lax.psum_scatter(
        jnp.dot(gated_out, w_out, preferred_element_type=jnp.float32).astype(jnp.bfloat16),
        "tp",
        scatter_dimension=0,
        tiled=True,
    )
    state_in, state_b, y_inter, y_full, layer_out = (state_in, state_b, y_inter, y_full, layer_out)
    dgated = lax.dot_general(
        lax.all_gather(cotangent, "tp", axis=0, tiled=True),
        w_out,
        (((1,), (1,)), ((), ())),
        preferred_element_type=jnp.float32,
    )
    dgated = dgated.reshape(nblocks, BLOCK, head_count, head_dim)
    grad_y = dgated * silu_z
    grad_w = (grad_y * exp_cum[..., None]).astype(jnp.bfloat16)
    injected = jnp.einsum("cqhp,cqn->chpn", grad_w, c_blocks, preferred_element_type=jnp.float32)
    adjoint_next = carried(block_decay, injected, True)
    dgated, grad_y, grad_w, adjoint_next = (dgated, grad_y, grad_w, adjoint_next)
    grad_gate = (dgated * y_full * (sigmoid_z + gate_float * sigmoid_z * (1.0 - sigmoid_z))).astype(
        jnp.bfloat16
    )
    grad_gate = grad_gate.reshape(tok_rows, feature_width)
    grad_y_b = grad_y.astype(jnp.bfloat16)
    adjoint_b = adjoint_next.astype(jnp.bfloat16)
    pair_dots = jnp.einsum(
        "cqhp,ckhp->chqk", grad_y_b, x_blocks, preferred_element_type=jnp.float32
    )
    dmix = pair_dots * decay_mat
    dmix_b = dmix.astype(jnp.bfloat16)
    state_dx = (
        jnp.einsum("ckn,chpn->ckhp", b_blocks, adjoint_b, preferred_element_type=jnp.float32)
        * tail_weight[..., None]
    )
    grad_inputs = (
        jnp.einsum("chqk,cqhp->ckhp", mixing_b, grad_y_b, preferred_element_type=jnp.float32)
        + state_dx
    )
    grad_inputs = grad_inputs.astype(jnp.bfloat16).reshape(tok_rows, feature_width)
    b_terms = jnp.einsum("chqk,cqn->ckn", dmix_b, c_blocks, preferred_element_type=jnp.float32)
    b_terms = b_terms + jnp.einsum(
        "ckhp,chpn->ckn", weighted, adjoint_b, preferred_element_type=jnp.float32
    )
    c_terms = jnp.einsum("chqk,ckn->cqn", dmix_b, b_blocks, preferred_element_type=jnp.float32)
    c_terms = c_terms + jnp.einsum(
        "cqhp,chpn->cqn", grad_w, state_b, preferred_element_type=jnp.float32
    )
    grad_b, grad_c = (
        lax.psum_scatter(
            b_terms.reshape(tok_rows, nstate).astype(jnp.bfloat16),
            "tp",
            scatter_dimension=0,
            tiled=True,
        ).astype(jnp.float32),
        lax.psum_scatter(
            c_terms.reshape(tok_rows, nstate).astype(jnp.bfloat16),
            "tp",
            scatter_dimension=0,
            tiled=True,
        ).astype(jnp.float32),
    )
    cross_terms = dmix * scores[:, None]
    decay_flow = jnp.transpose(jnp.sum(cross_terms, 3) - jnp.sum(cross_terms, 2), (0, 2, 1))
    outflow = jnp.sum(x_blocks.astype(jnp.float32) * state_dx, 3)
    decay_flow = decay_flow + jnp.sum(grad_y * y_inter, 3) - outflow
    closing = jnp.sum(outflow, 1) + block_decay * jnp.sum(adjoint_next * state_in, (2, 3))
    decay_flow = decay_flow.at[:, -1, :].add(closing)
    grad_decay = jnp.einsum("ut,cuh->cth", lower_ones, decay_flow, precision=lax.Precision.HIGHEST)
    grad_decay = jnp.transpose(grad_decay, (2, 0, 1)).reshape(head_count, tok_rows)
    return (layer_out, grad_inputs, grad_gate, grad_b, grad_c, grad_decay)


def solution(mesh):
    in_specs = (
        P("ctx", "tp"),
        P("ctx", "tp"),
        P("ctx", None),
        P("ctx", None),
        P("tp", "ctx"),
        P("tp", None),
        P(("ctx", "tp"), None),
    )
    out_specs = (
        P(("ctx", "tp"), None),
        P("ctx", "tp"),
        P("ctx", "tp"),
        P(("ctx", "tp"), None),
        P(("ctx", "tp"), None),
        P("tp", "ctx"),
    )
    return jax.shard_map(local, mesh=mesh, in_specs=in_specs, out_specs=out_specs, check_vma=False)
```

profile of v0, /device:TPU:8, one launch (start us, length us, event | category | flops | bytes accessed | tf_op | source)
XLA Modules:
  0.0 479.4 jit_solution(16107612873647827048)
XLA Ops:
  9.3 1.8 convolution_add_fusion.1
  11.4 32.1 %all-gather.7.cloned.1.call-done = bf16[128,4096]{1,0:T(8,128)(2,1)} async-done(((bf16[16,4096]{1,0:T(8,128)(2,1)}), bf16[128,4096]{1,0:T(8,128)(2,1)}) %all-gather.7.cloned.1.call-update) | async-done | bytes 1048592 | tf_op jit(solution)/shard_map/all_gather | solution.py:112
  43.5 4.0 fusion.39
  49.0 45.2 %all-gather = f32[64,1,4]{2,1,0:T(1,128)S(1)} all-gather(f32[1,1,4]{2,1,0:T(1,128)S(1)} %copy.53), channel_id=2, replica_groups=mesh['ctx'=64,'tp'=8] {'ctx'}, dimensions={0}, use_global_device_ids=true | all-gather | bytes 1040 | tf_op jit(solution)/shard_map/all_gather | solution.py:11
  95.1 91.4 %all-gather.9.cloned.1.call-done = f32[256,128,128]{2,1,0:T(8,128)} async-done(((f32[4,128,128]{2,1,0:T(8,128)}), f32[256,128,128]{2,1,0:T(8,128)}) %all-gather.9.cloned.1.call-update) | async-done | bytes 16777232 | tf_op jit(solution)/shard_map/all_gather | solution.py:11
  186.5 70.2 %while.21 = (s32[]{:T(128)}, f32[4,128,128]{2,1,0:T(8,128)S(1)}, s32[]{:T(128)}, f32[64,4]{1,0:T(8,128)S(1)}, f32[64,4,128,128]{3,2,1,0:T(8,128)}, /*index=5*/s32[]{:T(128)}, s32[]{:T(128)}) while((s32[]{:T(128)}, f32[4,128,128]{2,1,0:T(8,128)S(1)}, s32[]{:T(128)}, f32[64,4]{1,0:T(8,128)S(1)}, f32[64,4,128,128]{3,2,1,0:T(8,128)}, ...), condition=%wide.region_1.2_spmd.clone, body=%wide.region_0.1_spmd.clone.sunk | while | flops 262148 | bytes 786585 | solution.py:24
  201.8 1.1 fusion.59
  202.9 1.1 fusion.59
  210.5 1.1 fusion.59
  214.9 1.1 fusion.59
  217.1 1.1 fusion.59
  221.5 1.1 fusion.59
  224.8 1.1 fusion.59
  229.2 1.1 fusion.59
  243.4 1.1 fusion.59
  244.6 1.1 fusion.59
  252.3 1.1 fusion.59
  254.5 1.1 fusion.59
  255.6 1.1 fusion.59
  258.2 69.4 %all-gather.11.cloned.1.call-done = f32[256,128,128]{2,1,0:T(8,128)} async-done(((f32[4,128,128]{2,1,0:T(8,128)}), f32[256,128,128]{2,1,0:T(8,128)}) %all-gather.11.cloned.1.call-update) | async-done | bytes 16777232 | tf_op jit(solution)/shard_map/all_gather | solution.py:11
  327.6 70.8 %while.22 = (s32[]{:T(128)}, f32[4,128,128]{2,1,0:T(8,128)S(1)}, s32[]{:T(128)}, f32[64,4]{1,0:T(8,128)S(1)}, f32[64,4,128,128]{3,2,1,0:T(8,128)}, /*index=5*/s32[]{:T(128)}, s32[]{:T(128)}, s32[]{:T(128)}, s32[]{:T(128)}) while((s32[]{:T(128)}, f32[4,128,128]{2,1,0:T(8,128)S(1)}, s32[]{:T(128)}, f32[64,4]{1,0:T(8,128)S(1)}, ...), condition=%wide.region_4.5_spmd.clone, body=%wide.region_3.4_spmd.clone.sunk | while | flops 262152 | bytes 786647 | solution.py:24
  328.8 1.1 fusion.60
  336.5 1.1 fusion.60
  342.0 1.1 fusion.60
  343.2 1.1 fusion.60
  346.5 1.1 fusion.60
  347.6 1.1 fusion.60
  348.7 1.1 fusion.60
  352.0 1.1 fusion.60
  353.1 1.1 fusion.60
  354.2 1.1 fusion.60
  355.3 1.1 fusion.60
  357.6 1.1 fusion.60
  358.7 1.1 fusion.60
  359.8 1.1 fusion.60
  360.9 1.1 fusion.60
  363.1 1.1 fusion.60
  364.2 1.1 fusion.60
  369.8 1.1 fusion.60
  375.3 1.1 fusion.60
  383.0 1.1 fusion.60
  390.8 1.1 fusion.60
  396.3 1.1 fusion.60
  399.5 3.9 convolution_convert_fusion
  404.3 1.3 convert_element_type.112
  408.2 25.1 %reduce-scatter.6.cloned.1.call-done = bf16[16,128]{1,0:T(8,128)(2,1)} async-done(((bf16[128,128]{1,0:T(8,128)(2,1)}), bf16[16,128]{1,0:T(8,128)(2,1)}) %reduce-scatter.6.cloned.1.call-update) | async-done | bytes 4112 | tf_op jit(solution)/shard_map/reduce_scatter | solution.py:152
  433.3 1.3 convert_element_type.110
  434.5 38.0 %reduce-scatter.4.cloned.1.call-done = bf16[16,4096]{1,0:T(8,128)(2,1)} async-done(((bf16[128,4096]{1,0:T(8,128)(2,1)}), bf16[16,4096]{1,0:T(8,128)(2,1)}) %reduce-scatter.4.cloned.1.call-update) | async-done | bytes 131088 | tf_op jit(solution)/shard_map/reduce_scatter | solution.py:104
  (280 shorter events, 109.7 us)
Async XLA Ops:
  7.2 2.1 copy-start
  7.2 40.3 %copy-start.2 = (bf16[128,512]{1,0:T(8,128)(2,1)S(1)}, bf16[128,512]{1,0:T(8,128)(2,1)}, u32[]{:S(2)}) copy-start(bf16[128,512]{1,0:T(8,128)(2,1)} %param.14) | copy-start | bytes 393220
  7.2 36.3 %all-gather.7.cloned.1.call-start = ((), (), s32[]{:S(2)}) async-start(), calls=%async_computation.4 | async-start | bytes 1179648 | tf_op jit(solution)/shard_map/all_gather | solution.py:112
  7.9 178.5 %all-gather.9.cloned.1.call-start = ((), (), s32[]{:S(2)}) async-start(), calls=%async_computation.7 | async-start | bytes 17039360 | tf_op jit(solution)/shard_map/all_gather | solution.py:11
  9.1 38.5 %copy-start.3 = (bf16[128,128]{1,0:T(8,128)(2,1)S(1)}, bf16[128,128]{1,0:T(8,128)(2,1)}, u32[]{:S(2)}) copy-start(bf16[128,128]{1,0:T(8,128)(2,1)} %param.16) | copy-start | bytes 98308
  11.1 37.5 %copy-start.1 = (bf16[128,512]{1,0:T(8,128)(2,1)S(1)}, bf16[128,512]{1,0:T(8,128)(2,1)}, u32[]{:S(2)}) copy-start(bf16[128,512]{1,0:T(8,128)(2,1)} %param.13) | copy-start | bytes 393220
  11.2 316.5 %all-gather.11.cloned.1.call-start = ((), (), s32[]{:S(2)}) async-start(), calls=%async_computation.8 | async-start | bytes 17039360 | tf_op jit(solution)/shard_map/all_gather | solution.py:11
  48.6 355.7 %reduce-scatter.8.cloned.1.call-start = ((), (), s32[]{:S(2)}) async-start(), calls=%async_computation.6 | async-start | bytes 36864 | tf_op jit(solution)/shard_map/reduce_scatter | solution.py:158
  257.8 175.4 %reduce-scatter.6.cloned.1.call-start = ((), (), s32[]{:S(2)}) async-start(), calls=%async_computation.5 | async-start | bytes 36864 | tf_op jit(solution)/shard_map/reduce_scatter | solution.py:152
  399.5 73.1 %reduce-scatter.4.cloned.1.call-start = ((), (), s32[]{:S(2)}) async-start(), calls=%async_computation.3 | async-start | bytes 1179648 | tf_op jit(solution)/shard_map/reduce_scatter | solution.py:104
Sparse Core Ops, SparseCore 0:
  10.2 33.2 all-gather.6
  46.5 139.9 all-gather.8
  189.5 138.1 all-gather.10
  330.9 33.6 reduce-scatter.7
  399.6 33.5 reduce-scatter.5
  436.5 36.0 reduce-scatter.3
where the time goes:
time: 484 us; the launch traced here: 479 us
  waiting for transfers between devices  257 us (53%)
  other arithmetic  138 us (29%)
  blocking collectives  45.2 us (9%)
  matrix products  15.8 us (3%)
  between operations  14.3 us (3%)
    all_gather x2, waiting for transfers between devices, entering(): everything = jax.tree.map(lambda part: lax.all_gather(part, axis), shard)  161 us
    select_n x128, other arithmetic, lap(): return jax.tree.map(lambda a, b: jnp.where(reached, a, b), new, before)  135 us
    all_gather x1, blocking collectives, entering(): everything = jax.tree.map(lambda part: lax.all_gather(part, axis), shard)  45.2 us
    reduce_scatter x1, waiting for transfers between devices, local(): lax.psum_scatter(jnp.dot(gated_out, w_out, preferred_element_type=jnp.flo...  38 us
    all_gather x1, waiting for transfers between devices, local(): lax.all_gather(cotangent, 'tp', axis=0, tiled=True)  32.1 us
    reduce_scatter x1, waiting for transfers between devices, local(): lax.psum_scatter(b_terms.reshape(tok_rows, nstate).astype(jnp.bfloat16),...  25.1 us
  transfers between devices with their start and end apart: 6, of which 5 were waited for; matrix products, arithmetic and copies ran while one was open for 33% of the time, Pallas kernels for 0%

commit v1 on v0

--- a/solution.py
+++ b/solution.py
@@ -4,6 +4,11 @@
 from jax.sharding import PartitionSpec as P
 
 BLOCK = 128
+
+
+def tiled_gather(x, axis, dim):
+    copies = jnp.concatenate([x] * lax.axis_size(axis), axis=dim)
+    return lax.all_to_all(copies, axis, dim, dim, tiled=True)
 
 
 def entering(shard, axis, combine, identity, reverse):
@@ -109,7 +114,7 @@
     )
     state_in, state_b, y_inter, y_full, layer_out = (state_in, state_b, y_inter, y_full, layer_out)
     dgated = lax.dot_general(
-        lax.all_gather(cotangent, "tp", axis=0, tiled=True),
+        tiled_gather(cotangent, "tp", 0),
         w_out,
         (((1,), (1,)), ((), ())),
         preferred_element_type=jnp.float32,

time: 484 us -> 453 us (0.936)
  waiting for transfers between devices: 257 us -> 206 us
  local copies, waits for them, and re-layouts: 4.27 us -> 16.8 us
    all_gather x2, waiting for transfers between devices: 161 us -> 127 us  [entering(): everything = jax.tree.map(lambda part: lax.all_gather(part, axis), shard)]
    all_gather x1 -> x0, waiting for transfers between devices: 32.1 us -> none  [local(): lax.all_gather(cotangent, 'tp', axis=0, tiled=True)]
    all_to_all x0 -> x1, waiting for transfers between devices: none -> 15.7 us  [tiled_gather(): return lax.all_to_all(copies, axis, dim, dim, tiled=True)]
    unnamed x12 -> x19, local copies, waits for them, and re-layouts: 1.78 us -> 12.7 us
  transfers between devices with their start and end apart: 6 -> 6, of which waited for: 5 -> 5; matrix products, arithmetic and copies ran while one was open for 33% -> 37% of each run, Pallas kernels for 0% -> 0%
where the time goes in v1:
time: 453 us; the launch traced here: 448 us
  waiting for transfers between devices  206 us (45%)
  other arithmetic  138 us (30%)
  blocking collectives  48.8 us (11%)
  local copies, waits for them, and re-layouts  16.8 us (4%)
  matrix products  15.6 us (3%)
  between operations  14 us (3%)
  starting transfers between devices  4.64 us (1%)
    select_n x128, other arithmetic, lap(): return jax.tree.map(lambda a, b: jnp.where(reached, a, b), new, before)  135 us
    all_gather x2, waiting for transfers between devices, entering(): everything = jax.tree.map(lambda part: lax.all_gather(part, axis), shard)  127 us
    all_gather x1, blocking collectives, entering(): everything = jax.tree.map(lambda part: lax.all_gather(part, axis), shard)  48.8 us
    reduce_scatter x1, waiting for transfers between devices, local(): lax.psum_scatter(jnp.dot(gated_out, w_out, preferred_element_type=jnp.flo...  38.1 us
    reduce_scatter x1, waiting for transfers between devices, local(): lax.psum_scatter(b_terms.reshape(tok_rows, nstate).astype(jnp.bfloat16),...  25 us
    all_to_all x1, waiting for transfers between devices, tiled_gather(): return lax.all_to_all(copies, axis, dim, dim, tiled=True)  15.7 us
    unnamed x19, local copies, waits for them, and re-layouts  12.7 us
  transfers between devices with their start and end apart: 6, of which 5 were waited for; matrix products, arithmetic and copies ran while one was open for 37% of the time, Pallas kernels for 0%

profile of v1, /device:TPU:8, one launch (start us, length us, event | category | flops | bytes accessed | tf_op | source)
XLA Modules:
  0.0 448.3 jit_solution(10421244442179180765)
XLA Ops:
  8.5 1.8 convolution_add_fusion.1
  10.4 1.6 constant_dynamic-update-slice_fusion.7
  12.0 1.6 constant_dynamic-update-slice_fusion.6
  13.5 1.6 constant_dynamic-update-slice_fusion.5
  15.1 1.6 constant_dynamic-update-slice_fusion.4
  16.7 1.6 constant_dynamic-update-slice_fusion.3
  18.2 1.6 constant_dynamic-update-slice_fusion.2
  19.8 1.6 constant_dynamic-update-slice_fusion.1
  21.3 1.6 constant_dynamic-update-slice_fusion
  22.9 4.4 all-to-all-start
  27.6 15.7 %all-to-all-done = bf16[8,16,4096]{2,1,0:T(8,128)(2,1)S(1)} async-done(((bf16[8,16,4096]{2,1,0:T(8,128)(2,1)}), bf16[8,16,4096]{2,1,0:T(8,128)(2,1)S(1)}, u32[]{:S(2)}, u32[]{:S(2)}) %all-to-all-start) | async-done | bytes 1048608 | tf_op jit(solution)/shard_map/all_to_all | solution.py:11
  43.3 3.8 fusion.39
  48.6 48.8 %all-gather = f32[64,1,4]{2,1,0:T(1,128)S(1)} all-gather(f32[1,1,4]{2,1,0:T(1,128)S(1)} %copy.53), channel_id=2, replica_groups=mesh['ctx'=64,'tp'=8] {'ctx'}, dimensions={0}, use_global_device_ids=true | all-gather | bytes 1040 | tf_op jit(solution)/shard_map/all_gather | solution.py:16
  98.2 58.0 %all-gather.6.cloned.1.call-done = f32[256,128,128]{2,1,0:T(8,128)} async-done(((f32[4,128,128]{2,1,0:T(8,128)}), f32[256,128,128]{2,1,0:T(8,128)}) %all-gather.6.cloned.1.call-update) | async-done | bytes 16777232 | tf_op jit(solution)/shard_map/all_gather | solution.py:16
  156.2 70.4 %while.21 = (s32[]{:T(128)}, f32[4,128,128]{2,1,0:T(8,128)S(1)}, s32[]{:T(128)}, f32[64,4]{1,0:T(8,128)S(1)}, f32[64,4,128,128]{3,2,1,0:T(8,128)}, /*index=5*/s32[]{:T(128)}, s32[]{:T(128)}) while((s32[]{:T(128)}, f32[4,128,128]{2,1,0:T(8,128)S(1)}, s32[]{:T(128)}, f32[64,4]{1,0:T(8,128)S(1)}, f32[64,4,128,128]{3,2,1,0:T(8,128)}, ...), condition=%wide.region_1.2_spmd.clone, body=%wide.region_0.1_spmd.clone.sunk | while | flops 262148 | bytes 786593 | solution.py:29
  171.6 1.1 fusion.59
  172.7 1.1 fusion.59
  176.0 1.1 fusion.59
  179.3 1.1 fusion.59
  182.6 1.1 fusion.59
  187.0 1.1 fusion.59
  191.4 1.1 fusion.59
  194.7 1.1 fusion.59
  198.0 1.1 fusion.59
  199.1 1.1 fusion.59
  213.4 1.1 fusion.59
  221.1 1.1 fusion.59
  222.3 1.1 fusion.59
  224.5 1.1 fusion.59
  228.2 68.9 %all-gather.8.cloned.1.call-done = f32[256,128,128]{2,1,0:T(8,128)} async-done(((f32[4,128,128]{2,1,0:T(8,128)}), f32[256,128,128]{2,1,0:T(8,128)}) %all-gather.8.cloned.1.call-update) | async-done | bytes 16777232 | tf_op jit(solution)/shard_map/all_gather | solution.py:16
  297.1 70.6 %while.22 = (s32[]{:T(128)}, f32[4,128,128]{2,1,0:T(8,128)S(1)}, s32[]{:T(128)}, f32[64,4]{1,0:T(8,128)S(1)}, f32[64,4,128,128]{3,2,1,0:T(8,128)}, /*index=5*/s32[]{:T(128)}, s32[]{:T(128)}, s32[]{:T(128)}, s32[]{:T(128)}) while((s32[]{:T(128)}, f32[4,128,128]{2,1,0:T(8,128)S(1)}, s32[]{:T(128)}, f32[64,4]{1,0:T(8,128)S(1)}, ...), condition=%wide.region_4.5_spmd.clone, body=%wide.region_3.4_spmd.clone.sunk | while | flops 262152 | bytes 786655 | solution.py:29
  312.5 1.1 fusion.60
  315.9 1.1 fusion.60
  317.0 1.1 fusion.60
  318.1 1.1 fusion.60
  319.2 1.1 fusion.60
  321.4 1.1 fusion.60
  322.5 1.1 fusion.60
  323.6 1.1 fusion.60
  324.7 1.1 fusion.60
  328.0 1.1 fusion.60
  329.1 1.1 fusion.60
  333.5 1.1 fusion.60
  368.8 3.9 convolution_convert_fusion
  373.5 1.3 convert_element_type.112
  377.4 25.0 %reduce-scatter.6.cloned.1.call-done = bf16[16,128]{1,0:T(8,128)(2,1)} async-done(((bf16[128,128]{1,0:T(8,128)(2,1)}), bf16[16,128]{1,0:T(8,128)(2,1)}) %reduce-scatter.6.cloned.1.call-update) | async-done | bytes 4112 | tf_op jit(solution)/shard_map/reduce_scatter | solution.py:157
  402.4 1.3 convert_element_type.110
  403.7 38.1 %reduce-scatter.4.cloned.1.call-done = bf16[16,4096]{1,0:T(8,128)(2,1)} async-done(((bf16[128,4096]{1,0:T(8,128)(2,1)}), bf16[16,4096]{1,0:T(8,128)(2,1)}) %reduce-scatter.4.cloned.1.call-update) | async-done | bytes 131088 | tf_op jit(solution)/shard_map/reduce_scatter | solution.py:109
  (287 shorter events, 118.7 us)
Async XLA Ops:
  7.2 1.4 copy-start
  7.2 149.0 %all-gather.6.cloned.1.call-start = ((), (), s32[]{:S(2)}) async-start(), calls=%async_computation.7 | async-start | bytes 17039360 | tf_op jit(solution)/shard_map/all_gather | solution.py:16
  22.9 24.2 %copy-start.2 = (bf16[128,512]{1,0:T(8,128)(2,1)S(1)}, bf16[128,512]{1,0:T(8,128)(2,1)}, u32[]{:S(2)}) copy-start(bf16[128,512]{1,0:T(8,128)(2,1)} %param.14) | copy-start | bytes 393220
  22.9 24.3 %copy-start.3 = (bf16[128,128]{1,0:T(8,128)(2,1)S(1)}, bf16[128,128]{1,0:T(8,128)(2,1)}, u32[]{:S(2)}) copy-start(bf16[128,128]{1,0:T(8,128)(2,1)} %param.16) | copy-start | bytes 98308
  22.9 20.4 %all-to-all-start = ((bf16[8,16,4096]{2,1,0:T(8,128)(2,1)}), bf16[8,16,4096]{2,1,0:T(8,128)(2,1)S(1)}, u32[]{:S(2)}, u32[]{:S(2)}) async-start(bf16[8,16,4096]{2,1,0:T(8,128)(2,1)} %bitcast.23), calls=%async_computation.1 | async-start | bytes 2097152 | tf_op jit(solution)/shard_map/all_to_all | solution.py:11
  27.3 20.9 %copy-start.1 = (bf16[128,512]{1,0:T(8,128)(2,1)S(1)}, bf16[128,512]{1,0:T(8,128)(2,1)}, u32[]{:S(2)}) copy-start(bf16[128,512]{1,0:T(8,128)(2,1)} %param.13) | copy-start | bytes 393220
  27.4 269.7 %all-gather.8.cloned.1.call-start = ((), (), s32[]{:S(2)}) async-start(), calls=%async_computation.8 | async-start | bytes 17039360 | tf_op jit(solution)/shard_map/all_gather | solution.py:16
  48.2 325.3 %reduce-scatter.8.cloned.1.call-start = ((), (), s32[]{:S(2)}) async-start(), calls=%async_computation.6 | async-start | bytes 36864 | tf_op jit(solution)/shard_map/reduce_scatter | solution.py:163
  227.8 174.6 %reduce-scatter.6.cloned.1.call-start = ((), (), s32[]{:S(2)}) async-start(), calls=%async_computation.5 | async-start | bytes 36864 | tf_op jit(solution)/shard_map/reduce_scatter | solution.py:157
  368.7 73.1 %reduce-scatter.4.cloned.1.call-start = ((), (), s32[]{:S(2)}) async-start(), calls=%async_computation.4 | async-start | bytes 1179648 | tf_op jit(solution)/shard_map/reduce_scatter | solution.py:109
Sparse Core Ops, SparseCore 0:
  11.0 145.1 all-gather.5
  159.2 137.8 all-gather.7
  300.5 33.6 reduce-scatter.7
  368.8 33.5 reduce-scatter.5
  405.7 36.1 reduce-scatter.3
